TPU v7x, 32 devices: a whole 2x2x4 slice. The times are simulated.
32 devices in a mesh: dp: 8 (over z, x), expert: 4 (over y, core).
Axes of the slice: x: 2, y: 2, z: 4, core: 2. Of those that a mesh axis runs over, the one named last changes fastest.
Arguments:
- tokens: bfloat16 [8192, 768], P(('dp', 'expert')), may hold values from -6 to 6
- expert_ids: int32 [8192, 2], P(('dp', 'expert')), may hold values from 0 to 15, all different within a row; in each aligned block of 256 rows (0 to 255, 256 to 511, ...) at most 64 rows name the same one
- gate_fixed: int32 [8192, 2], P(('dp', 'expert')), may hold values from 8192 to 65535
- cotangent: bfloat16 [8192, 768], P(('dp', 'expert')), may hold values from -6 to 6
- w_gate: bfloat16 [16, 768, 384], P('expert'), may hold values from -0.21875 to 0.21875
- w_up: bfloat16 [16, 768, 384], P('expert'), may hold values from -0.21875 to 0.21875
- w_down: bfloat16 [16, 768, 384], P('expert'), may hold values from -0.3125 to 0.3125
Outputs:
- layer_out: bfloat16 [8192, 768], P(('dp', 'expert'))
- input_grad: bfloat16 [8192, 768], P(('dp', 'expert'))
- grad_gate: float32 [16, 768, 384], P('expert', 'dp')
- grad_up: float32 [16, 768, 384], P('expert', 'dp')
- grad_down: float32 [16, 768, 384], P('expert', 'dp')
Inputs may be any that keep to these rules, and one draw needn't show every extreme that they name: `expert_ids`: A row names 2 different experts. In each aligned block of 256 rows (the rows of one device) no expert is named by more than 64 rows, and in some block one expert is named by exactly 64 rows.
All inputs are finite; a program needn't handle non-finite values.
Results may differ from a plain program's by a relative error of at most 0.015.
Values may be sent and summed in bfloat16 or wider, within the bound.
A program may use at most 64 MiB of HBM per device.

v0:
```python
import functools

import jax
import jax.numpy as jnp
from jax import lax
from jax.experimental import pallas as pl
from jax.experimental.pallas import tpu as pltpu
from jax.sharding import PartitionSpec as P

BF = jnp.bfloat16
F32 = jnp.float32


def dot(a, b, ca=1, cb=0):
    return lax.dot_general(a, b, (((ca,), (cb,)), ((), ())), preferred_element_type=F32)


def flipped(me, k):
    out, bit = me, 1
    while bit <= k:
        if k & bit:
            out = out + bit * (1 - 2 * lax.rem(lax.div(me, bit), 2))
        bit *= 2
    return out


def kernel(
    n, inner, outer, top,
    meta, tok, cot, wg_h, wu_h, wd_h,
    act_o, grad_o,
    w, meta_r, tok_r, cot_r, hot, slot_gate, xs, gs, hs, pre, ys, ds, y_t, y_r, parts,
    w_sem, ms_sem, mr_sem, ts_sem, tr_sem, cs_sem, cr_sem, ys_sem, yr_sem, xs_sem, xr_sem, zs_sem, zr_sem,
    x_r, z_s, z_r,
):
    me = lax.axis_index("expert")
    my_dp = lax.axis_index("dp")
    my_z = lax.div(my_dp, inner)
    my_x = lax.rem(my_dp, inner)
    other_x = 1 - my_x
    partner_dp = my_z * inner + other_x
    local, d_model, ff = w.shape[1:]
    tokens = tok.shape[0]
    cap = slot_gate.shape[2]
    rows = parts.shape[4]

    loads = [pltpu.make_async_copy(h, w.at[i], w_sem.at[i]) for i, h in enumerate((wg_h, wu_h, wd_h))]

    barrier = pltpu.get_barrier_semaphore()
    for k in range(1, n):
        pl.semaphore_signal(barrier, inc=1, device_id={"expert": flipped(me, k)})
    pl.semaphore_signal(barrier, inc=1, device_id={"dp": partner_dp})
    for k in range(1, outer):
        pl.semaphore_signal(barrier, inc=1, device_id={"dp": flipped(my_z, k) * inner + my_x})
    pl.semaphore_wait(barrier, (n - 1) + 1 + (outer - 1))

    def send(src, dst, s, r, **where):
        return pltpu.make_async_remote_copy(src_ref=src, dst_ref=dst, send_sem=s, recv_sem=r, device_id=where)

    def meta_copy(k):
        return send(meta, meta_r.at[k], ms_sem.at[k], mr_sem.at[k], expert=flipped(me, k))

    def rows_copy(own, landed, s, r, k):
        if k % 2 == 0 or k == 1:
            return send(own, landed.at[k], s.at[k], r.at[k], expert=flipped(me, k))
        return send(landed.at[k - 1], landed.at[k], s.at[k], r.at[k], expert=flipped(me, 1))

    def tok_copy(k):
        return rows_copy(tok, tok_r, ts_sem, tr_sem, k)

    def cot_copy(k):
        return rows_copy(cot, cot_r, cs_sem, cr_sem, k)

    for k in range(1, n):
        meta_copy(k).start()
    direct = [k for k in range(2, n, 2)] + [1]
    for k in direct:
        tok_copy(k).start()
    for k in direct:
        cot_copy(k).start()
    for c in loads:
        c.start()

    above = (
        lax.broadcasted_iota(jnp.int32, (tokens, tokens), 0)
        < lax.broadcasted_iota(jnp.int32, (tokens, tokens), 1)
    )
    before = jnp.where(above, 1.0, 0.0).astype(BF)
    padded = -(-local // 8) * 8

    def route(k):
        if k:
            meta_copy(k).wait_recv()
            mv = meta_r[k]
        else:
            mv = meta[...]
        expert = lax.broadcasted_iota(jnp.int32, (padded, tokens), 0) + me * local
        hit = jnp.zeros((padded, tokens), F32)
        gate = jnp.zeros((padded, tokens), F32)
        for c in range(top):
            same = mv[c : c + 1] == expert
            hit = hit + jnp.where(same, 1.0, 0.0)
            gate = gate + jnp.where(same, mv[top + c : top + c + 1].astype(F32) * (1.0 / 65536.0), 0.0)
        rank = dot(hit.astype(BF), before)
        rank = jnp.where(hit > 0.5, rank, -1.0)
        slot = lax.broadcasted_iota(jnp.int32, (cap, tokens), 0).astype(F32)
        for i in range(local):
            picked = jnp.where(slot == rank[i : i + 1], 1.0, 0.0)
            hot[k, i * cap : (i + 1) * cap] = picked.astype(BF)
            value = jnp.sum(picked * gate[i : i + 1], axis=1, keepdims=True)
            slot_gate[k, i] = jnp.broadcast_to(value, (cap, 128))

    def take_tokens(k, block):
        got = dot(hot[k], block).astype(BF)
        for i in range(local):
            xs[i, k * cap : (k + 1) * cap] = got[i * cap : (i + 1) * cap]

    def take_grads(k, block):
        got = dot(hot[k], block)
        for i in range(local):
            gs[i, k * cap : (k + 1) * cap] = (
                slot_gate[k, i][:, :1] * got[i * cap : (i + 1) * cap]
            ).astype(BF)

    def arrive(copy_of, take, landed):
        for k in range(2, n, 2):
            copy_of(k).wait_recv()
            copy_of(k + 1).start()
        for k in range(1, n):
            if k % 2 or k == 1:
                copy_of(k).wait_recv()
            take(k, landed[k])

    def x_copy(e, a):
        return send(
            parts.at[other_x, e, a], x_r.at[e, a], xs_sem.at[e, a], xr_sem.at[e, a], dp=partner_dp
        )

    def z_copy(k, e, a):
        there = flipped(my_z, k)
        return send(
            z_s.at[e, a, there], z_r.at[k, e, a], zs_sem.at[k, e, a], zr_sem.at[k, e, a],
            dp=there * inner + my_x,
        )

    def put(e, a, value):
        for zz in range(outer):
            for xx in range(inner):
                at = (zz * inner + xx) * rows
                parts[xx, e, a, zz] = value[at : at + rows].astype(BF)
        x_copy(e, a).start()

    def forward(e, carry):
        x = xs[e]
        pre_gate = dot(x, w[0, e])
        pre_up = dot(x, w[1, e])
        pre[0, e] = pre_gate
        pre[1, e] = pre_up
        hidden = (pre_gate * jax.nn.sigmoid(pre_gate) * pre_up).astype(BF)
        hs[e] = hidden
        o = dot(hidden, w[2, e], 1, 1).astype(BF).astype(F32)
        for k in range(n):
            ys[k, e] = (slot_gate[k, e][:, :1] * o[k * cap : (k + 1) * cap]).astype(BF)
        return carry

    def backward(e, carry):
        x, g = xs[e], gs[e]
        put(e, 2, dot(g, hs[e], 0, 0))
        hidden_grad = dot(g, w[2, e])
        pre_gate, pre_up = pre[0, e], pre[1, e]
        sig = jax.nn.sigmoid(pre_gate)
        up_grad = (hidden_grad * (pre_gate * sig)).astype(BF)
        put(e, 1, dot(x, up_grad, 0, 0))
        gate_grad = (hidden_grad * pre_up * sig * (1.0 + pre_gate * (1.0 - sig))).astype(BF)
        put(e, 0, dot(x, gate_grad, 0, 0))
        back = dot(gate_grad, w[0, e], 1, 1) + dot(up_grad, w[1, e], 1, 1)
        back = back.astype(BF)
        for k in range(n):
            ds[k, e] = back[k * cap : (k + 1) * cap]
        return carry

    for k in range(n):
        route(k)
    take_tokens(0, tok[...])
    take_grads(0, cot[...])
    arrive(tok_copy, take_tokens, tok_r)
    for c in loads:
        c.wait()
    lax.fori_loop(0, local, forward, 0)
    arrive(cot_copy, take_grads, cot_r)
    lax.fori_loop(0, local, backward, 0)

    def y_copy(j, k):
        return send(y_t.at[j, k], y_r.at[j, k], ys_sem.at[j, k], yr_sem.at[j, k], expert=flipped(me, k))

    def spread(j, k):
        src = (ys, ds)[j]
        return dot(hot[k], src[k].reshape(local * cap, d_model), 0, 0)

    def x_stage(e, carry):
        for a in (2, 1, 0):
            x_copy(e, a).wait_recv()
            z_s[e, a] = (parts[my_x, e, a].astype(F32) + x_r[e, a].astype(F32)).astype(BF)
            for k in range(1, outer):
                z_copy(k, e, a).start()
        return carry

    def finish(e, carry):
        for a in (2, 1, 0):
            total = z_s[e, a, my_z].astype(F32)
            for k in range(1, outer):
                z_copy(k, e, a).wait_recv()
                total = total + z_r[k, e, a].astype(F32)
            grad_o[a, e] = total
        return carry

    def returned(j):
        total = spread(j, 0)
        for k in range(1, n):
            y_copy(j, k).wait_recv()
            total = total + y_r[j, k].astype(F32)
        act_o[j] = total.astype(BF)

    x_stage(0, 0)
    for j in range(2):
        for k in range(n - 1, 0, -1):
            y_t[j, k] = spread(j, k).astype(BF)
            y_copy(j, k).start()
    lax.fori_loop(1, local - 1, x_stage, 0)
    for j in range(2):
        returned(j)
    lax.fori_loop(0, local - 2, finish, 0)
    x_stage(local - 1, 0)
    finish(local - 2, 0)
    finish(local - 1, 0)

    for k in range(1, n):
        meta_copy(k).wait_send()
        tok_copy(k).wait_send()
        cot_copy(k).wait_send()
        for j in range(2):
            y_copy(j, k).wait_send()

    def drain(e, carry):
        for a in range(3):
            x_copy(e, a).wait_send()
            for k in range(1, outer):
                z_copy(k, e, a).wait_send()
        return carry

    lax.fori_loop(0, local, drain, 0)


def write(scale, act, grad, out_o, din_o, gg_o, gu_o, gd_o):
    out_o[...] = act[0]
    din_o[...] = act[1]
    for a, o in enumerate((gg_o, gu_o, gd_o)):
        o[...] = grad[a] * scale


def shards(tokens, expert_ids, gate_fixed, cotangent, w_gate, w_up, w_down):
    n = lax.axis_size("expert")
    replicas = lax.axis_size("dp")
    inner = 2
    outer = replicas // inner
    local, d_model, ff = w_gate.shape
    count, top = expert_ids.shape
    cap = count * top * 2 // (local * n)
    rows = d_model // replicas
    scale = float(count * n * replicas * top // (local * n)) ** (-0.5)
    meta = jnp.concatenate(
        [expert_ids.T, gate_fixed.T, jnp.zeros((8 - 2 * top, count), jnp.int32)], axis=0
    )
    vmem = pl.BlockSpec(memory_space=pltpu.VMEM)
    hbm = pl.BlockSpec(memory_space=pl.ANY)
    dma = pltpu.SemaphoreType.DMA
    half = pltpu.VMEM((local, 3, outer, rows, ff), BF)
    act, grad = pl.pallas_call(
        functools.partial(kernel, n, inner, outer, top),
        out_shape=(
            jax.ShapeDtypeStruct((2, count, d_model), BF),
            jax.ShapeDtypeStruct((3, local, rows, ff), F32),
        ),
        in_specs=[vmem] * 3 + [hbm] * 3,
        out_specs=(vmem,) * 2,
        scratch_shapes=[
            pltpu.VMEM((3, local, d_model, ff), BF),
            pltpu.VMEM((n, 8, count), jnp.int32),
            pltpu.VMEM((n, count, d_model), BF),
            pltpu.VMEM((n, count, d_model), BF),
            pltpu.VMEM((n, local * cap, count), BF),
            pltpu.VMEM((n, local, cap, 128), F32),
            pltpu.VMEM((local, n * cap, d_model), BF),
            pltpu.VMEM((local, n * cap, d_model), BF),
            pltpu.VMEM((local, n * cap, ff), BF),
            pltpu.VMEM((2, local, n * cap, ff), F32),
            pltpu.VMEM((n, local, cap, d_model), BF),
            pltpu.VMEM((n, local, cap, d_model), BF),
            pltpu.VMEM((2, n, count, d_model), BF),
            pltpu.VMEM((2, n, count, d_model), BF),
            pltpu.VMEM((inner, local, 3, outer, rows, ff), BF),
            dma((3,)),
            dma((n,)), dma((n,)), dma((n,)), dma((n,)), dma((n,)), dma((n,)),
            dma((2, n)), dma((2, n)),
            dma((local, 3)), dma((local, 3)),
            dma((outer, local, 3)), dma((outer, local, 3)),
            half, half, pltpu.VMEM((outer, local, 3, rows, ff), BF),
        ],
        compiler_params=pltpu.CompilerParams(
            collective_id=0, has_side_effects=True, vmem_limit_bytes=60 * 1024 * 1024
        ),
    )(meta, tokens, cotangent, w_gate, w_up, w_down)
    step = count // local
    act_block = jax.ShapeDtypeStruct((count, d_model), BF)
    grad_block = jax.ShapeDtypeStruct((local, rows, ff), F32)
    return pl.pallas_call(
        functools.partial(write, scale),
        out_shape=(act_block, act_block, grad_block, grad_block, grad_block),
        in_specs=[vmem] * 2,
        out_specs=(vmem,) * 5,
    )(act, grad)


def solution(mesh):
    return jax.shard_map(
        shards,
        mesh=mesh,
        in_specs=(P(("dp", "expert"), None),) * 4 + (P("expert", None, None),) * 3,
        out_specs=(P(("dp", "expert"), None),) * 2 + (P("expert", "dp", None),) * 3,
        check_vma=False,
    )
```

profile of v0, /device:TPU:0, one launch (start us, length us, event | category | flops | bytes accessed | tf_op | source)
XLA Modules:
  0.0 121.1 jit_solution(1208867945972647649)
XLA Ops:
  0.6 0.1 pad.2.clone
  0.7 1.4 %add_add_fusion.meta = s32[8,256]{1,0:T(8,128)} fusion(s32[2,256]{1,0:T(2,128)} %bitcast.2, s32[2,256]{1,0:T(2,128)} %bitcast.3, s32[8]{0:T(128)S(1)} %pad.2.clone), kind=kLoop, calls=%fused_computation | loop fusion | flops 4096 | bytes 12320 | tf_op jit(solution)/shard_map/concatenate | solution.py:270
  2.1 115.7 %shard_map.110 = (bf16[2,256,768]{2,1,0:T(8,128)(2,1)}, f32[3,4,96,384]{3,2,1,0:T(8,128)}) custom-call(s32[8,256]{1,0:T(8,128)} %add_add_fusion.meta, bf16[256,768]{1,0:T(8,128)(2,1)} %tok.1, bf16[256,768]{1,0:T(8,128)(2,1)} %cot.1, bf16[4,768,384]{2,1,0:T(8,128)(2,1)} %wg_h.1, bf16[4,768,384]{2,1,0:T(8,128)(2,1)} %wu_h.1, bf16[4,768,384]{2,1,0:T(8,128)(2,1)} %wd_h.1), custom_call_target="tpu_custom_call" | custom-call | tf_op jit(solution)/shard_map/pallas_call | solution.py:277
  117.8 3.3 %shard_map.111 = (bf16[256,768]{1,0:T(8,128)(2,1)}, bf16[256,768]{1,0:T(8,128)(2,1)}, f32[4,96,384]{2,1,0:T(8,128)}, f32[4,96,384]{2,1,0:T(8,128)}, f32[4,96,384]{2,1,0:T(8,128)}) custom-call(bf16[2,256,768]{2,1,0:T(8,128)(2,1)} %get-tuple-element.7.act, f32[3,4,96,384]{3,2,1,0:T(8,128)} %get-tuple-element.8.grad), custom_call_target="tpu_custom_call" | custom-call | tf_op jit(solution)/shard_map/pallas_call | solution.py:315
  (1 shorter events, 0.0 us)
where the time goes:
time: 121 us
  Pallas kernels  119 us (98%)
  other arithmetic  1.37 us (1%)
    pallas_call x1, Pallas kernels, shards(): pl.pallas_call(functools.partial(kernel, n, inner, outer, top), out_shape...  116 us
    pallas_call x1, Pallas kernels, shards(): pl.pallas_call(functools.partial(write, scale), out_shape=(act_block, act...  3.25 us

commit v1 on v0

v1 whole, which is shorter than its diff:
```python
import functools

import jax
import jax.numpy as jnp
from jax import lax
from jax.experimental import pallas as pl
from jax.experimental.pallas import tpu as pltpu
from jax.sharding import PartitionSpec as P

BF = jnp.bfloat16
F32 = jnp.float32


def dot(a, b, ca=1, cb=0):
    return lax.dot_general(a, b, (((ca,), (cb,)), ((), ())), preferred_element_type=F32)


def flipped(me, k):
    out, bit = me, 1
    while bit <= k:
        if k & bit:
            out = out + bit * (1 - 2 * lax.rem(lax.div(me, bit), 2))
        bit *= 2
    return out


def kernel(
    n, inner, outer, top,
    ids, gates, tok, cot, wg_h, wu_h, wd_h,
    act_o, grad_o,
    wgu, wd, ids_r, gates_r, rows_r, hot, hot1, slot_gate, slot_gate1,
    xs, gs, xs1, gs1, hs, hs1, pre, gu, gu1, ys, ds, y_r, parts, x_r, z_s, z_r,
    w_sem, ms_sem, mr_sem, gs_sem, gr_sem, ys_sem, yr_sem, xs_sem, xr_sem, zs_sem, zr_sem,
):
    me = lax.axis_index("expert")
    my_dp = lax.axis_index("dp")
    my_z = lax.div(my_dp, inner)
    my_x = lax.rem(my_dp, inner)
    my_zh = lax.div(my_z, 2)
    my_zl = lax.rem(my_z, 2)
    other_x = 1 - my_x
    partner_dp = my_z * inner + other_x
    mate_dp = flipped(my_z, 1) * inner + my_x
    local, d_model, ff2 = wgu.shape
    ff = ff2 // 2
    part = local // 2
    mine = my_zl * part
    tokens = tok.shape[0]
    split = tokens // 2
    cap = slot_gate.shape[2]
    rows = parts.shape[4]
    groups = outer // 2
    own = (tok, cot)

    loads = [
        pltpu.make_async_copy(wg_h, wgu.at[:, :, pl.ds(0, ff)], w_sem.at[0]),
        pltpu.make_async_copy(wu_h, wgu.at[:, :, pl.ds(ff, ff)], w_sem.at[1]),
        pltpu.make_async_copy(wd_h, wd, w_sem.at[2]),
    ]

    barrier = pltpu.get_barrier_semaphore()
    for k in range(1, n):
        pl.semaphore_signal(barrier, inc=1, device_id={"expert": flipped(me, k)})
    for k in range(1, n):
        pl.semaphore_signal(barrier, inc=1, device_id={"dp": mate_dp, "expert": flipped(me, k)})
    pl.semaphore_signal(barrier, inc=1, device_id={"dp": partner_dp})
    for k in range(1, outer):
        pl.semaphore_signal(barrier, inc=1, device_id={"dp": flipped(my_z, k) * inner + my_x})
    pl.semaphore_wait(barrier, 2 * (n - 1) + 1 + (outer - 1))

    def send(src, dst, s, r, **where):
        return pltpu.make_async_remote_copy(src_ref=src, dst_ref=dst, send_sem=s, recv_sem=r, device_id=where)

    def meta_copies(s, k):
        where = {"expert": flipped(me, k)} if k else {}
        if s:
            where["dp"] = mate_dp
        return [
            send(a, b.at[s, k], ms_sem.at[i, s, k], mr_sem.at[i, s, k], **where)
            for i, (a, b) in enumerate(((ids, ids_r), (gates, gates_r)))
        ]

    def row_copies(t, s, k, halves=(0, 1)):
        sems = lambda h: (gs_sem.at[t, s, k, h], gr_sem.at[t, s, k, h])
        landed = rows_r.at[t, s, k]
        if s == 0:
            if k % 2 and k > 1:
                return [send(rows_r.at[t, 0, k - 1], landed, *sems(0), expert=flipped(me, 1))]
            return [send(own[t], landed, *sems(0), expert=flipped(me, k))]
        if k == 0:
            return [send(own[t], landed, *sems(0), dp=mate_dp)]
        if k % 2:
            return [send(rows_r.at[t, 1, k - 1], landed, *sems(0), expert=flipped(me, 1))]
        span = (pl.ds(0, split), pl.ds(split, tokens - split))
        src = (rows_r.at[t, 0, k], rows_r.at[t, 1, 0])
        where = ({"dp": mate_dp}, {"expert": flipped(me, k)})
        return [send(src[h].at[span[h]], landed.at[span[h]], *sems(h), **where[h]) for h in halves]

    def start(copies):
        for c in copies:
            c.start()

    def landed(copies):
        for c in copies:
            c.wait_recv()

    def left(copies):
        for c in copies:
            c.wait_send()

    pairs = [(0, k) for k in range(1, n)] + [(1, k) for k in range(n)]
    for s, k in pairs:
        start(meta_copies(s, k))
    direct = [(0, k) for k in range(2, n, 2)] + [(1, 0), (0, 1)]
    for t in range(2):
        for s, k in direct:
            start(row_copies(t, s, k))
    for c in loads:
        c.start()

    above = (
        lax.broadcasted_iota(jnp.int32, (tokens, tokens), 0)
        < lax.broadcasted_iota(jnp.int32, (tokens, tokens), 1)
    )
    before = jnp.where(above, 1.0, 0.0).astype(BF)
    padded = -(-local // 8) * 8

    def route(s, k):
        if s or k:
            landed(meta_copies(s, k))
            iv, gv = ids_r[s, k], gates_r[s, k]
        else:
            iv, gv = ids[...], gates[...]
        count, first = (part, me * local + mine) if s else (local, me * local)
        hots, values = (hot1, slot_gate1) if s else (hot, slot_gate)
        expert = lax.broadcasted_iota(jnp.int32, (padded, tokens), 0) + first
        hit = jnp.zeros((padded, tokens), F32)
        gate = jnp.zeros((padded, tokens), F32)
        for c in range(top):
            same = iv[c : c + 1] == expert
            hit = hit + jnp.where(same, 1.0, 0.0)
            gate = gate + jnp.where(same, gv[c : c + 1].astype(F32) * (1.0 / 65536.0), 0.0)
        rank = dot(hit.astype(BF), before)
        rank = jnp.where(hit > 0.5, rank, -1.0)
        slot = lax.broadcasted_iota(jnp.int32, (cap, tokens), 0).astype(F32)
        for i in range(count):
            picked = jnp.where(slot == rank[i : i + 1], 1.0, 0.0)
            hots[k, i * cap : (i + 1) * cap] = picked.astype(BF)
            value = jnp.sum(picked * gate[i : i + 1], axis=1, keepdims=True)
            values[k, i] = jnp.broadcast_to(value, (cap, 128))

    def take(t, s, k):
        block = own[t][...] if s == 0 and k == 0 else rows_r[t, s, k]
        got = dot((hot1 if s else hot)[k], block)
        count = part if s else local
        into = ((xs, gs), (xs1, gs1))[s][t]
        for i in range(count):
            value = got[i * cap : (i + 1) * cap]
            if t:
                value = (slot_gate1 if s else slot_gate)[k, i][:, :1] * value
            into[i, k * cap : (k + 1) * cap] = value.astype(BF)

    def x_copy(i, a, j):
        zz = pl.ds(2 * flipped(my_zh, j), 2)
        return send(
            parts.at[other_x, i, a, zz], x_r.at[i, a, zz], xs_sem.at[i, a, j], xr_sem.at[i, a, j], dp=partner_dp
        )

    def z_copy(k, i, a):
        there = flipped(my_z, k)
        return send(
            z_s.at[i, a, there], z_r.at[k, i, a], zs_sem.at[k, i, a], zr_sem.at[k, i, a],
            dp=there * inner + my_x,
        )

    def put(i, a, value):
        for zz in range(outer):
            for xx in range(inner):
                at = (zz * inner + xx) * rows
                parts[xx, i, a, zz] = value[at : at + rows].astype(BF)
        for j in range(groups - 1, 0, -1):
            x_copy(i, a, j).start()

    def grads(hidden_grad, p, into, e):
        pre_gate, pre_up = p[:, :ff], p[:, ff:]
        sig = jax.nn.sigmoid(pre_gate)
        into[e, :, ff:] = (hidden_grad * (pre_gate * sig)).astype(BF)
        into[e, :, :ff] = (hidden_grad * pre_up * sig * (1.0 + pre_gate * (1.0 - sig))).astype(BF)

    def forward(e, carry):
        p = dot(xs[e], wgu[e])
        pre[e] = p
        pre_gate, pre_up = p[:, :ff], p[:, ff:]
        hidden = (pre_gate * jax.nn.sigmoid(pre_gate) * pre_up).astype(BF)
        hs[e] = hidden
        o = dot(hidden, wd[e], 1, 1).astype(BF).astype(F32)
        for k in range(n):
            ys[k, e] = (slot_gate[k, e][:, :1] * o[k * cap : (k + 1) * cap]).astype(BF)
        return carry

    def backward(e, carry):
        grads(dot(gs[e], wd[e]), pre[e], gu, e)
        back = dot(gu[e], wgu[e], 1, 1).astype(BF)
        for k in range(n):
            ds[k, e] = back[k * cap : (k + 1) * cap]
        return carry

    def forward_pair(i, carry):
        p = dot(xs1[i], wgu[mine + i])
        pre[i] = p
        pre_gate, pre_up = p[:, :ff], p[:, ff:]
        hs1[i] = (pre_gate * jax.nn.sigmoid(pre_gate) * pre_up).astype(BF)
        return carry

    def backward_pair(i, carry):
        e = mine + i
        put(i, 2, dot(gs[e], hs[e], 0, 0) + dot(gs1[i], hs1[i], 0, 0))
        grads(dot(gs1[i], wd[e]), pre[i], gu1, i)
        both = dot(xs[e], gu[e], 0, 0) + dot(xs1[i], gu1[i], 0, 0)
        put(i, 0, both[:, :ff])
        put(i, 1, both[:, ff:])
        return carry

    def y_copy(j, k):
        return send(rows_r.at[j, 0, k], y_r.at[j, k], ys_sem.at[j, k], yr_sem.at[j, k], expert=flipped(me, k))

    def spread(j, k):
        src = (ys, ds)[j]
        return dot(hot[k], src[k].reshape(local * cap, d_model), 0, 0)

    def back_out(j):
        for k in range(n - 1, 0, -1):
            if k % 2 == 0:
                left(row_copies(j, 0, k + 1) + row_copies(j, 1, k, (0,)))
            rows_r[j, 0, k] = spread(j, k).astype(BF)
            y_copy(j, k).start()

    def returned(j):
        total = spread(j, 0)
        for k in range(1, n):
            y_copy(j, k).wait_recv()
            total = total + y_r[j, k].astype(F32)
        act_o[j] = total.astype(BF)

    even = range(2, n, 2)

    def relay(t):
        for k in even:
            landed(row_copies(t, 0, k))
            start(row_copies(t, 0, k + 1))
            start(row_copies(t, 1, k, (0,)))
        landed(row_copies(t, 1, 0))
        for k in even:
            start(row_copies(t, 1, k, (1,)))
        start(row_copies(t, 1, 1))
        for k in even:
            take(t, 0, k)
        take(t, 1, 0)
        for k in even:
            landed(row_copies(t, 0, k + 1))
            take(t, 0, k + 1)
        landed(row_copies(t, 1, 1))
        take(t, 1, 1)

    def relay_far(t):
        for k in even:
            landed(row_copies(t, 1, k))
            start(row_copies(t, 1, k + 1))
            take(t, 1, k)
        for k in even:
            landed(row_copies(t, 1, k + 1))
            take(t, 1, k + 1)

    route(0, 0)
    for t in range(2):
        take(t, 0, 0)
    for s, k in pairs:
        route(s, k)
    for t in range(2):
        landed(row_copies(t, 0, 1))
        take(t, 0, 1)
    relay(0)
    for c in loads:
        c.wait()
    lax.fori_loop(0, local, forward, 0)
    relay(1)
    lax.fori_loop(0, local, backward, 0)
    relay_far(0)
    lax.fori_loop(0, part, forward_pair, 0)
    back_out(0)
    relay_far(1)
    lax.fori_loop(0, part, backward_pair, 0)

    def near(i, carry):
        for a in (2, 0, 1):
            x_copy(i, a, 0).start()
        return carry

    lax.fori_loop(0, part, near, 0)
    back_out(1)

    def x_stage(j):
        def stage(i, carry):
            for a in (2, 0, 1):
                x_copy(i, a, j).wait_recv()
                for low in range(2):
                    zz = 2 * flipped(my_zh, j) + low
                    z_s[i, a, zz] = (parts[my_x, i, a, zz].astype(F32) + x_r[i, a, zz].astype(F32)).astype(BF)
                for low in range(2):
                    if 2 * j + low:
                        z_copy(2 * j + low, i, a).start()
            return carry

        return stage

    for j in range(groups - 1, 0, -1):
        lax.fori_loop(0, part, x_stage(j), 0)
    returned(0)
    lax.fori_loop(0, part, x_stage(0), 0)
    returned(1)

    def finish(i, carry):
        for a in (2, 0, 1):
            total = z_s[i, a, my_z].astype(F32)
            for k in range(2, outer, 2):
                z_copy(k, i, a).wait_recv()
                total = total + z_r[k, i, a].astype(F32)
            grad_o[a, mine + i] = total
            z_copy(1, i, a).wait_recv()
            total = z_r[1, i, a].astype(F32)
            for k in range(3, outer, 2):
                z_copy(k, i, a).wait_recv()
                total = total + z_r[k, i, a].astype(F32)
            grad_o[a, part - mine + i] = total
        return carry

    lax.fori_loop(0, part, finish, 0)

    for s, k in pairs:
        left(meta_copies(s, k))
        for t in range(2):
            if s or k < 2 or k % 2 == 0:
                left(row_copies(t, s, k, (1,)))
    for j in range(2):
        for k in range(1, n):
            y_copy(j, k).wait_send()

    def drain(i, carry):
        for a in range(3):
            for j in range(groups):
                x_copy(i, a, j).wait_send()
            for k in range(1, outer):
                z_copy(k, i, a).wait_send()
        return carry

    lax.fori_loop(0, part, drain, 0)


def write(scale, act, grad, out_o, din_o, gg_o, gu_o, gd_o):
    out_o[...] = act[0]
    din_o[...] = act[1]
    for a, o in enumerate((gg_o, gu_o, gd_o)):
        o[...] = grad[a] * scale


def shards(tokens, expert_ids, gate_fixed, cotangent, w_gate, w_up, w_down):
    n = lax.axis_size("expert")
    replicas = lax.axis_size("dp")
    inner = 2
    outer = replicas // inner
    local, d_model, ff = w_gate.shape
    count, top = expert_ids.shape
    cap = count * top * 2 // (local * n)
    rows = d_model // replicas
    part = local // 2
    scale = float(count * n * replicas * top // (local * n)) ** (-0.5)
    vmem = pl.BlockSpec(memory_space=pltpu.VMEM)
    hbm = pl.BlockSpec(memory_space=pl.ANY)
    dma = pltpu.SemaphoreType.DMA
    slots = n * cap
    act, grad = pl.pallas_call(
        functools.partial(kernel, n, inner, outer, top),
        out_shape=(
            jax.ShapeDtypeStruct((2, count, d_model), BF),
            jax.ShapeDtypeStruct((3, local, rows, ff), F32),
        ),
        in_specs=[vmem] * 4 + [hbm] * 3,
        out_specs=(vmem,) * 2,
        scratch_shapes=[
            pltpu.VMEM((local, d_model, 2 * ff), BF),
            pltpu.VMEM((local, d_model, ff), BF),
            pltpu.VMEM((2, n, top, count), jnp.int32),
            pltpu.VMEM((2, n, top, count), jnp.int32),
            pltpu.VMEM((2, 2, n, count, d_model), BF),
            pltpu.VMEM((n, local * cap, count), BF),
            pltpu.VMEM((n, part * cap, count), BF),
            pltpu.VMEM((n, local, cap, 128), F32),
            pltpu.VMEM((n, part, cap, 128), F32),
            pltpu.VMEM((local, slots, d_model), BF),
            pltpu.VMEM((local, slots, d_model), BF),
            pltpu.VMEM((part, slots, d_model), BF),
            pltpu.VMEM((part, slots, d_model), BF),
            pltpu.VMEM((local, slots, ff), BF),
            pltpu.VMEM((part, slots, ff), BF),
            pltpu.VMEM((local, slots, 2 * ff), F32),
            pltpu.VMEM((local, slots, 2 * ff), BF),
            pltpu.VMEM((part, slots, 2 * ff), BF),
            pltpu.VMEM((n, local, cap, d_model), BF),
            pltpu.VMEM((n, local, cap, d_model), BF),
            pltpu.VMEM((2, n, count, d_model), BF),
            pltpu.VMEM((inner, part, 3, outer, rows, ff), BF),
            pltpu.VMEM((part, 3, outer, rows, ff), BF),
            pltpu.VMEM((part, 3, outer, rows, ff), BF),
            pltpu.VMEM((outer, part, 3, rows, ff), BF),
            dma((3,)),
            dma((2, 2, n)), dma((2, 2, n)),
            dma((2, 2, n, 2)), dma((2, 2, n, 2)),
            dma((2, n)), dma((2, n)),
            dma((part, 3, outer // 2)), dma((part, 3, outer // 2)),
            dma((outer, part, 3)), dma((outer, part, 3)),
        ],
        compiler_params=pltpu.CompilerParams(
            collective_id=0, has_side_effects=True, vmem_limit_bytes=60 * 1024 * 1024
        ),
    )(expert_ids.T, gate_fixed.T, tokens, cotangent, w_gate, w_up, w_down)
    act_block = jax.ShapeDtypeStruct((count, d_model), BF)
    grad_block = jax.ShapeDtypeStruct((local, rows, ff), F32)
    return pl.pallas_call(
        functools.partial(write, scale),
        out_shape=(act_block, act_block, grad_block, grad_block, grad_block),
        in_specs=[vmem] * 2,
        out_specs=(vmem,) * 5,
    )(act, grad)


def solution(mesh):
    return jax.shard_map(
        shards,
        mesh=mesh,
        in_specs=(P(("dp", "expert"), None),) * 4 + (P("expert", None, None),) * 3,
        out_specs=(P(("dp", "expert"), None),) * 2 + (P("expert", "dp", None),) * 3,
        check_vma=False,
    )
```

time: 121 us -> 90.6 us (0.75)
  Pallas kernels: 119 us -> 89.8 us
  other arithmetic: 1.37 us -> 0 us
    pallas_call x1, Pallas kernels: 116 us -> 86.6 us  [shards(): pl.pallas_call(functools.partial(kernel, n, inner, outer, top), out_shape...]
    concatenate x1 -> x0, other arithmetic: 1.37 us -> none  [shards(): jnp.concatenate([expert_ids.T, gate_fixed.T, jnp.zeros((8 - 2 * top, coun...]
where the time goes in v1:
time: 90.6 us; the launch traced here: 90.5 us
  Pallas kernels  89.8 us (99%)
    pallas_call x1, Pallas kernels, shards(): pl.pallas_call(functools.partial(kernel, n, inner, outer, top), out_shape...  86.6 us
    pallas_call x1, Pallas kernels, shards(): pl.pallas_call(functools.partial(write, scale), out_shape=(act_block, act...  3.25 us

profile of v1, /device:TPU:0, one launch (start us, length us, event | category | flops | bytes accessed | tf_op | source)
XLA Modules:
  0.0 90.5 jit_solution(17478603104121868356)
XLA Ops:
  0.6 86.6 %shard_map.110 = (bf16[2,256,768]{2,1,0:T(8,128)(2,1)}, f32[3,4,96,384]{3,2,1,0:T(8,128)}) custom-call(s32[2,256]{1,0:T(2,128)} %bitcast.2, s32[2,256]{1,0:T(2,128)} %bitcast.3, bf16[256,768]{1,0:T(8,128)(2,1)} %tok.1, bf16[256,768]{1,0:T(8,128)(2,1)} %cot.1, bf16[4,768,384]{2,1,0:T(8,128)(2,1)} %wg_h.1, bf16[4,768,384]{2,1,0:T(8,128)(2,1)} %wu_h.1, ...), custom_call_target="tpu_custom_call" | custom-call | tf_op jit(solution)/shard_map/pallas_call | solution.py:381
  87.2 3.3 %shard_map.111 = (bf16[256,768]{1,0:T(8,128)(2,1)}, bf16[256,768]{1,0:T(8,128)(2,1)}, f32[4,96,384]{2,1,0:T(8,128)}, f32[4,96,384]{2,1,0:T(8,128)}, f32[4,96,384]{2,1,0:T(8,128)}) custom-call(bf16[2,256,768]{2,1,0:T(8,128)(2,1)} %get-tuple-element.7.act, f32[3,4,96,384]{3,2,1,0:T(8,128)} %get-tuple-element.8.grad), custom_call_target="tpu_custom_call" | custom-call | tf_op jit(solution)/shard_map/pallas_call | solution.py:428

commit v2 on v1

--- a/solution.py
+++ b/solution.py
@@ -9,6 +9,7 @@
 
 BF = jnp.bfloat16
 F32 = jnp.float32
+MARGIN = 6 * 1024 * 1024
 
 
 def dot(a, b, ca=1, cb=0):
@@ -25,12 +26,12 @@
 
 
 def kernel(
-    n, inner, outer, top,
-    ids, gates, tok, cot, wg_h, wu_h, wd_h,
+    n, inner, outer, top, scale,
+    ids_h, gates_h, tok_h, cot_h, wg_h, wu_h, wd_h,
     act_o, grad_o,
-    wgu, wd, ids_r, gates_r, rows_r, hot, hot1, slot_gate, slot_gate1,
+    act_s, grad_s, wgu, wd, ids_r, gates_r, rows_r, hot, hot1, slot_gate, slot_gate1,
     xs, gs, xs1, gs1, hs, hs1, pre, gu, gu1, ys, ds, y_r, parts, x_r, z_s, z_r,
-    w_sem, ms_sem, mr_sem, gs_sem, gr_sem, ys_sem, yr_sem, xs_sem, xr_sem, zs_sem, zr_sem,
+    w_sem, in_sem, out_sem, ms_sem, mr_sem, gs_sem, gr_sem, ys_sem, yr_sem, xs_sem, xr_sem, zs_sem, zr_sem,
 ):
     me = lax.axis_index("expert")
     my_dp = lax.axis_index("dp")
@@ -45,13 +46,19 @@
     ff = ff2 // 2
     part = local // 2
     mine = my_zl * part
-    tokens = tok.shape[0]
+    tokens = rows_r.shape[3]
     split = tokens // 2
     cap = slot_gate.shape[2]
     rows = parts.shape[4]
-    groups = outer // 2
-    own = (tok, cot)
-
+
+    inputs = [
+        pltpu.make_async_copy(src, dst, in_sem.at[i])
+        for i, (src, dst) in enumerate(
+            ((ids_h, ids_r.at[0, 0]), (gates_h, gates_r.at[0, 0]), (tok_h, rows_r.at[0, 0, 0]), (cot_h, rows_r.at[1, 0, 0]))
+        )
+    ]
+    for c in inputs:
+        c.start()
     loads = [
         pltpu.make_async_copy(wg_h, wgu.at[:, :, pl.ds(0, ff)], w_sem.at[0]),
         pltpu.make_async_copy(wu_h, wgu.at[:, :, pl.ds(ff, ff)], w_sem.at[1]),
@@ -76,8 +83,8 @@
         if s:
             where["dp"] = mate_dp
         return [
-            send(a, b.at[s, k], ms_sem.at[i, s, k], mr_sem.at[i, s, k], **where)
-            for i, (a, b) in enumerate(((ids, ids_r), (gates, gates_r)))
+            send(a.at[0, 0], a.at[s, k], ms_sem.at[i, s, k], mr_sem.at[i, s, k], **where)
+            for i, a in enumerate((ids_r, gates_r))
         ]
 
     def row_copies(t, s, k, halves=(0, 1)):
@@ -86,9 +93,9 @@
         if s == 0:
             if k % 2 and k > 1:
                 return [send(rows_r.at[t, 0, k - 1], landed, *sems(0), expert=flipped(me, 1))]
-            return [send(own[t], landed, *sems(0), expert=flipped(me, k))]
+            return [send(rows_r.at[t, 0, 0], landed, *sems(0), expert=flipped(me, k))]
         if k == 0:
-            return [send(own[t], landed, *sems(0), dp=mate_dp)]
+            return [send(rows_r.at[t, 0, 0], landed, *sems(0), dp=mate_dp)]
         if k % 2:
             return [send(rows_r.at[t, 1, k - 1], landed, *sems(0), expert=flipped(me, 1))]
         span = (pl.ds(0, split), pl.ds(split, tokens - split))
@@ -108,6 +115,8 @@
         for c in copies:
             c.wait_send()
 
+    for c in inputs:
+        c.wait()
     pairs = [(0, k) for k in range(1, n)] + [(1, k) for k in range(n)]
     for s, k in pairs:
         start(meta_copies(s, k))
@@ -128,9 +137,7 @@
     def route(s, k):
         if s or k:
             landed(meta_copies(s, k))
-            iv, gv = ids_r[s, k], gates_r[s, k]
-        else:
-            iv, gv = ids[...], gates[...]
+        iv, gv = ids_r[s, k], gates_r[s, k]
         count, first = (part, me * local + mine) if s else (local, me * local)
         hots, values = (hot1, slot_gate1) if s else (hot, slot_gate)
         expert = lax.broadcasted_iota(jnp.int32, (padded, tokens), 0) + first
@@ -150,8 +157,7 @@
             values[k, i] = jnp.broadcast_to(value, (cap, 128))
 
     def take(t, s, k):
-        block = own[t][...] if s == 0 and k == 0 else rows_r[t, s, k]
-        got = dot((hot1 if s else hot)[k], block)
+        got = dot((hot1 if s else hot)[k], rows_r[t, s, k])
         count = part if s else local
         into = ((xs, gs), (xs1, gs1))[s][t]
         for i in range(count):
@@ -160,10 +166,10 @@
                 value = (slot_gate1 if s else slot_gate)[k, i][:, :1] * value
             into[i, k * cap : (k + 1) * cap] = value.astype(BF)
 
-    def x_copy(i, a, j):
-        zz = pl.ds(2 * flipped(my_zh, j), 2)
+    def x_copy(i, a, k):
+        zz = flipped(my_z, k)
         return send(
-            parts.at[other_x, i, a, zz], x_r.at[i, a, zz], xs_sem.at[i, a, j], xr_sem.at[i, a, j], dp=partner_dp
+            parts.at[other_x, i, a, zz], x_r.at[i, a, zz], xs_sem.at[i, a, k], xr_sem.at[i, a, k], dp=partner_dp
         )
 
     def z_copy(k, i, a):
@@ -178,8 +184,8 @@
             for xx in range(inner):
                 at = (zz * inner + xx) * rows
                 parts[xx, i, a, zz] = value[at : at + rows].astype(BF)
-        for j in range(groups - 1, 0, -1):
-            x_copy(i, a, j).start()
+        for k in range(outer - 1, 1, -1):
+            x_copy(i, a, k).start()
 
     def grads(hidden_grad, p, into, e):
         pre_gate, pre_up = p[:, :ff], p[:, ff:]
@@ -207,18 +213,9 @@
 
     def forward_pair(i, carry):
         p = dot(xs1[i], wgu[mine + i])
-        pre[i] = p
+        pre[mine + i] = p
         pre_gate, pre_up = p[:, :ff], p[:, ff:]
         hs1[i] = (pre_gate * jax.nn.sigmoid(pre_gate) * pre_up).astype(BF)
-        return carry
-
-    def backward_pair(i, carry):
-        e = mine + i
-        put(i, 2, dot(gs[e], hs[e], 0, 0) + dot(gs1[i], hs1[i], 0, 0))
-        grads(dot(gs1[i], wd[e]), pre[i], gu1, i)
-        both = dot(xs[e], gu[e], 0, 0) + dot(xs1[i], gu1[i], 0, 0)
-        put(i, 0, both[:, :ff])
-        put(i, 1, both[:, ff:])
         return carry
 
     def y_copy(j, k):
@@ -235,12 +232,36 @@
             rows_r[j, 0, k] = spread(j, k).astype(BF)
             y_copy(j, k).start()
 
+    def act_copy(j):
+        return pltpu.make_async_copy(act_s.at[j], act_o.at[j], out_sem.at[j])
+
+    def grad_copy(a, i):
+        return pltpu.make_async_copy(grad_s.at[a, i], grad_o.at[a, i], out_sem.at[2 + a * local + i])
+
     def returned(j):
         total = spread(j, 0)
         for k in range(1, n):
             y_copy(j, k).wait_recv()
             total = total + y_r[j, k].astype(F32)
-        act_o[j] = total.astype(BF)
+        act_s[j] = total.astype(BF)
+        act_copy(j).start()
+
+    def x_stage(i, a, k):
+        zz = flipped(my_z, k)
+        x_copy(i, a, k).wait_recv()
+        z_s[i, a, zz] = (parts[my_x, i, a, zz].astype(F32) + x_r[i, a, zz].astype(F32)).astype(BF)
+        if k:
+            z_copy(k, i, a).start()
+
+    def finish(i, a):
+        for first, e in ((0, mine + i), (1, part - mine + i)):
+            total = 0.0
+            for k in range(first, outer, 2):
+                if k:
+                    z_copy(k, i, a).wait_recv()
+                total = total + (z_r[k, i, a] if k else z_s[i, a, my_z]).astype(F32)
+            grad_s[a, e] = total * scale
+            grad_copy(a, e).start()
 
     even = range(2, n, 2)
 
@@ -262,11 +283,13 @@
         landed(row_copies(t, 1, 1))
         take(t, 1, 1)
 
-    def relay_far(t):
+    def far_first(t):
         for k in even:
             landed(row_copies(t, 1, k))
             start(row_copies(t, 1, k + 1))
             take(t, 1, k)
+
+    def far_last(t):
         for k in even:
             landed(row_copies(t, 1, k + 1))
             take(t, 1, k + 1)
@@ -284,57 +307,47 @@
         c.wait()
     lax.fori_loop(0, local, forward, 0)
     relay(1)
-    lax.fori_loop(0, local, backward, 0)
-    relay_far(0)
+    lax.fori_loop(mine, mine + 1, backward, 0)
+    far_first(0)
+    lax.fori_loop(mine + 1, mine + part, backward, 0)
+    back_out(0)
+    far_last(0)
     lax.fori_loop(0, part, forward_pair, 0)
-    back_out(0)
-    relay_far(1)
-    lax.fori_loop(0, part, backward_pair, 0)
-
-    def near(i, carry):
-        for a in (2, 0, 1):
-            x_copy(i, a, 0).start()
-        return carry
-
-    lax.fori_loop(0, part, near, 0)
+    far_first(1)
+    lax.fori_loop(part - mine, local - mine, backward, 0)
+    far_last(1)
+
+    order = (2, 0, 1)
+    for i in range(part):
+        e = mine + i
+        put(i, 2, dot(gs[e], hs[e], 0, 0) + dot(gs1[i], hs1[i], 0, 0))
+        grads(dot(gs1[i], wd[e]), pre[e], gu1, i)
+        if i == part - 1:
+            for k in range(outer - 1, 1, -1):
+                x_stage(0, 2, k)
+        both = dot(xs[e], gu[e], 0, 0) + dot(xs1[i], gu1[i], 0, 0)
+        put(i, 0, both[:, :ff])
+        put(i, 1, both[:, ff:])
+
+    for k in (1, 0):
+        for i in range(part):
+            for a in order:
+                x_copy(i, a, k).start()
     back_out(1)
-
-    def x_stage(j):
-        def stage(i, carry):
-            for a in (2, 0, 1):
-                x_copy(i, a, j).wait_recv()
-                for low in range(2):
-                    zz = 2 * flipped(my_zh, j) + low
-                    z_s[i, a, zz] = (parts[my_x, i, a, zz].astype(F32) + x_r[i, a, zz].astype(F32)).astype(BF)
-                for low in range(2):
-                    if 2 * j + low:
-                        z_copy(2 * j + low, i, a).start()
-            return carry
-
-        return stage
-
-    for j in range(groups - 1, 0, -1):
-        lax.fori_loop(0, part, x_stage(j), 0)
+    for i in range(part):
+        for a in order:
+            if i or a != 2:
+                for k in range(outer - 1, 1, -1):
+                    x_stage(i, a, k)
     returned(0)
-    lax.fori_loop(0, part, x_stage(0), 0)
+    for i in range(part):
+        for a in order:
+            x_stage(i, a, 1)
     returned(1)
-
-    def finish(i, carry):
-        for a in (2, 0, 1):
-            total = z_s[i, a, my_z].astype(F32)
-            for k in range(2, outer, 2):
-                z_copy(k, i, a).wait_recv()
-                total = total + z_r[k, i, a].astype(F32)
-            grad_o[a, mine + i] = total
-            z_copy(1, i, a).wait_recv()
-            total = z_r[1, i, a].astype(F32)
-            for k in range(3, outer, 2):
-                z_copy(k, i, a).wait_recv()
-                total = total + z_r[k, i, a].astype(F32)
-            grad_o[a, part - mine + i] = total
-        return carry
-
-    lax.fori_loop(0, part, finish, 0)
+    for i in range(part):
+        for a in order:
+            x_stage(i, a, 0)
+            finish(i, a)
 
     for s, k in pairs:
         left(meta_copies(s, k))
@@ -347,20 +360,38 @@
 
     def drain(i, carry):
         for a in range(3):
-            for j in range(groups):
-                x_copy(i, a, j).wait_send()
-            for k in range(1, outer):
-                z_copy(k, i, a).wait_send()
+            for k in range(outer):
+                x_copy(i, a, k).wait_send()
+                if k:
+                    z_copy(k, i, a).wait_send()
         return carry
 
     lax.fori_loop(0, part, drain, 0)
-
-
-def write(scale, act, grad, out_o, din_o, gg_o, gu_o, gd_o):
-    out_o[...] = act[0]
-    din_o[...] = act[1]
-    for a, o in enumerate((gg_o, gu_o, gd_o)):
-        o[...] = grad[a] * scale
+    for j in range(2):
+        act_copy(j).wait()
+    for a in range(3):
+        for e in range(local):
+            grad_copy(a, e).wait()
+
+
+def write(act, grad, out_o, din_o, gg_o, gu_o, gd_o, sem):
+    srcs = (act.at[0], act.at[1], grad.at[0], grad.at[1], grad.at[2])
+    copies = [
+        pltpu.make_async_copy(src, dst, sem.at[i]) for i, (src, dst) in enumerate(zip(srcs, (out_o, din_o, gg_o, gu_o, gd_o)))
+    ]
+    for c in copies:
+        c.start()
+    for c in copies:
+        c.wait()
+
+
+def padded_bytes(ref):
+    size = jnp.dtype(ref.dtype).itemsize
+    *lead, high, low = ref.shape
+    total = size * (-(-high * size // 32) * 32 // size) * (-(-low // 128) * 128)
+    for extent in lead:
+        total *= extent
+    return total
 
 
 def shards(tokens, expert_ids, gate_fixed, cotangent, w_gate, w_up, w_down):
@@ -374,62 +405,70 @@
     rows = d_model // replicas
     part = local // 2
     scale = float(count * n * replicas * top // (local * n)) ** (-0.5)
-    vmem = pl.BlockSpec(memory_space=pltpu.VMEM)
     hbm = pl.BlockSpec(memory_space=pl.ANY)
     dma = pltpu.SemaphoreType.DMA
     slots = n * cap
+    buffers = [
+        pltpu.VMEM((2, count, d_model), BF),
+        pltpu.VMEM((3, local, rows, ff), F32),
+        pltpu.VMEM((local, d_model, 2 * ff), BF),
+        pltpu.VMEM((local, d_model, ff), BF),
+        pltpu.VMEM((2, n, top, count), jnp.int32),
+        pltpu.VMEM((2, n, top, count), jnp.int32),
+        pltpu.VMEM((2, 2, n, count, d_model), BF),
+        pltpu.VMEM((n, local * cap, count), BF),
+        pltpu.VMEM((n, part * cap, count), BF),
+        pltpu.VMEM((n, local, cap, 128), F32),
+        pltpu.VMEM((n, part, cap, 128), F32),
+        pltpu.VMEM((local, slots, d_model), BF),
+        pltpu.VMEM((local, slots, d_model), BF),
+        pltpu.VMEM((part, slots, d_model), BF),
+        pltpu.VMEM((part, slots, d_model), BF),
+        pltpu.VMEM((local, slots, ff), BF),
+        pltpu.VMEM((part, slots, ff), BF),
+        pltpu.VMEM((local, slots, 2 * ff), F32),
+        pltpu.VMEM((local, slots, 2 * ff), BF),
+        pltpu.VMEM((part, slots, 2 * ff), BF),
+        pltpu.VMEM((n, local, cap, d_model), BF),
+        pltpu.VMEM((n, local, cap, d_model), BF),
+        pltpu.VMEM((2, n, count, d_model), BF),
+        pltpu.VMEM((inner, part, 3, outer, rows, ff), BF),
+        pltpu.VMEM((part, 3, outer, rows, ff), BF),
+        pltpu.VMEM((part, 3, outer, rows, ff), BF),
+        pltpu.VMEM((outer, part, 3, rows, ff), BF),
+    ]
+    args = (expert_ids.T, gate_fixed.T, tokens, cotangent, w_gate, w_up, w_down)
     act, grad = pl.pallas_call(
-        functools.partial(kernel, n, inner, outer, top),
+        functools.partial(kernel, n, inner, outer, top, scale),
         out_shape=(
             jax.ShapeDtypeStruct((2, count, d_model), BF),
             jax.ShapeDtypeStruct((3, local, rows, ff), F32),
         ),
-        in_specs=[vmem] * 4 + [hbm] * 3,
-        out_specs=(vmem,) * 2,
-        scratch_shapes=[
-            pltpu.VMEM((local, d_model, 2 * ff), BF),
-            pltpu.VMEM((local, d_model, ff), BF),
-            pltpu.VMEM((2, n, top, count), jnp.int32),
-            pltpu.VMEM((2, n, top, count), jnp.int32),
-            pltpu.VMEM((2, 2, n, count, d_model), BF),
-            pltpu.VMEM((n, local * cap, count), BF),
-            pltpu.VMEM((n, part * cap, count), BF),
-            pltpu.VMEM((n, local, cap, 128), F32),
-            pltpu.VMEM((n, part, cap, 128), F32),
-            pltpu.VMEM((local, slots, d_model), BF),
-            pltpu.VMEM((local, slots, d_model), BF),
-            pltpu.VMEM((part, slots, d_model), BF),
-            pltpu.VMEM((part, slots, d_model), BF),
-            pltpu.VMEM((local, slots, ff), BF),
-            pltpu.VMEM((part, slots, ff), BF),
-            pltpu.VMEM((local, slots, 2 * ff), F32),
-            pltpu.VMEM((local, slots, 2 * ff), BF),
-            pltpu.VMEM((part, slots, 2 * ff), BF),
-            pltpu.VMEM((n, local, cap, d_model), BF),
-            pltpu.VMEM((n, local, cap, d_model), BF),
-            pltpu.VMEM((2, n, count, d_model), BF),
-            pltpu.VMEM((inner, part, 3, outer, rows, ff), BF),
-            pltpu.VMEM((part, 3, outer, rows, ff), BF),
-            pltpu.VMEM((part, 3, outer, rows, ff), BF),
-            pltpu.VMEM((outer, part, 3, rows, ff), BF),
-            dma((3,)),
+        in_specs=[hbm] * 7,
+        out_specs=(hbm,) * 2,
+        scratch_shapes=buffers + [
+            dma((3,)), dma((4,)), dma((2 + 3 * local,)),
             dma((2, 2, n)), dma((2, 2, n)),
             dma((2, 2, n, 2)), dma((2, 2, n, 2)),
             dma((2, n)), dma((2, n)),
-            dma((part, 3, outer // 2)), dma((part, 3, outer // 2)),
+            dma((part, 3, outer)), dma((part, 3, outer)),
             dma((outer, part, 3)), dma((outer, part, 3)),
         ],
         compiler_params=pltpu.CompilerParams(
-            collective_id=0, has_side_effects=True, vmem_limit_bytes=60 * 1024 * 1024
+            collective_id=0,
+            has_side_effects=True,
+            vmem_limit_bytes=min(sum(map(padded_bytes, buffers)) + MARGIN, 62 * 1024 * 1024),
         ),
-    )(expert_ids.T, gate_fixed.T, tokens, cotangent, w_gate, w_up, w_down)
+    )(*(pltpu.with_memory_space_constraint(v, pltpu.HBM) for v in args))
     act_block = jax.ShapeDtypeStruct((count, d_model), BF)
     grad_block = jax.ShapeDtypeStruct((local, rows, ff), F32)
     return pl.pallas_call(
-        functools.partial(write, scale),
+        write,
         out_shape=(act_block, act_block, grad_block, grad_block, grad_block),
-        in_specs=[vmem] * 2,
-        out_specs=(vmem,) * 5,
+        in_specs=[hbm] * 2,
+        out_specs=(hbm,) * 5,
+        scratch_shapes=[dma((5,))],
+        compiler_params=pltpu.CompilerParams(vmem_limit_bytes=1024 * 1024),
     )(act, grad)
 
 

time: 90.6 us -> 83.9 us (0.926)
  Pallas kernels: 89.8 us -> 83 us
    pallas_call x2, Pallas kernels: 89.8 us -> 83 us  [the longest x1 81.5 us: shards(): pl.pallas_call(functools.partial(kernel, n, inner, outer, top, scale), ou...]
where the time goes in v2:
time: 83.9 us; the launch traced here: 83.8 us
  Pallas kernels  83 us (99%)
    pallas_call x1, Pallas kernels, shards(): pl.pallas_call(functools.partial(kernel, n, inner, outer, top, scale), ou...  81.5 us

profile of v2, /device:TPU:0, one launch (start us, length us, event | category | flops | bytes accessed | tf_op | source)
XLA Modules:
  0.0 83.8 jit_solution(15139953231917291912)
XLA Ops:
  0.6 81.5 %shard_map.110 = (bf16[2,256,768]{2,1,0:T(8,128)(2,1)S(1)}, f32[3,4,96,384]{3,2,1,0:T(8,128)S(1)}) custom-call(s32[2,256]{1,0:T(2,128)} %bitcast.2, s32[2,256]{1,0:T(2,128)} %bitcast.3, bf16[256,768]{1,0:T(8,128)(2,1)} %tok_h.1, bf16[256,768]{1,0:T(8,128)(2,1)} %cot_h.1, bf16[4,768,384]{2,1,0:T(8,128)(2,1)} %wg_h.1, bf16[4,768,384]{2,1,0:T(8,128)(2,1)} %wu_h.1, ...), custom_call_target="tpu_custom_call" | custom-call | tf_op jit(solution)/shard_map/pallas_call | solution.py:441
  82.1 1.5 %shard_map.111 = (bf16[256,768]{1,0:T(8,128)(2,1)}, bf16[256,768]{1,0:T(8,128)(2,1)}, f32[4,96,384]{2,1,0:T(8,128)}, f32[4,96,384]{2,1,0:T(8,128)}, f32[4,96,384]{2,1,0:T(8,128)}) custom-call(bf16[2,256,768]{2,1,0:T(8,128)(2,1)S(1)} %get-tuple-element.7.act, f32[3,4,96,384]{3,2,1,0:T(8,128)S(1)} %get-tuple-element.8.grad), custom_call_target="tpu_custom_call" | custom-call | tf_op jit(solution)/shard_map/pallas_call | solution.py:465

commit v3 on v2

--- a/solution.py
+++ b/solution.py
@@ -29,7 +29,7 @@
     n, inner, outer, top, scale,
     ids_h, gates_h, tok_h, cot_h, wg_h, wu_h, wd_h,
     act_o, grad_o,
-    act_s, grad_s, wgu, wd, ids_r, gates_r, rows_r, hot, hot1, slot_gate, slot_gate1,
+    act_s, grad_s, wgu, wd, meta_r, rows_r, hot, hot1, slot_gate, slot_gate1,
     xs, gs, xs1, gs1, hs, hs1, pre, gu, gu1, ys, ds, y_r, parts, x_r, z_s, z_r,
     w_sem, in_sem, out_sem, ms_sem, mr_sem, gs_sem, gr_sem, ys_sem, yr_sem, xs_sem, xr_sem, zs_sem, zr_sem,
 ):
@@ -54,7 +54,12 @@
     inputs = [
         pltpu.make_async_copy(src, dst, in_sem.at[i])
         for i, (src, dst) in enumerate(
-            ((ids_h, ids_r.at[0, 0]), (gates_h, gates_r.at[0, 0]), (tok_h, rows_r.at[0, 0, 0]), (cot_h, rows_r.at[1, 0, 0]))
+            (
+                (ids_h, meta_r.at[0, pl.ds(0, top)]),
+                (gates_h, meta_r.at[0, pl.ds(top, top)]),
+                (tok_h, rows_r.at[0, 0, 0]),
+                (cot_h, rows_r.at[1, 0, 0]),
+            )
         )
     ]
     for c in inputs:
@@ -78,17 +83,20 @@
     def send(src, dst, s, r, **where):
         return pltpu.make_async_remote_copy(src_ref=src, dst_ref=dst, send_sem=s, recv_sem=r, device_id=where)
 
-    def meta_copies(s, k):
+    def meta_copy(s, k):
         where = {"expert": flipped(me, k)} if k else {}
         if s:
             where["dp"] = mate_dp
-        return [
-            send(a.at[0, 0], a.at[s, k], ms_sem.at[i, s, k], mr_sem.at[i, s, k], **where)
-            for i, a in enumerate((ids_r, gates_r))
-        ]
+        return send(meta_r.at[0], meta_r.at[s * n + k], ms_sem.at[0], mr_sem.at[0], **where)
+
+    others = pl.ds(1, 2 * n - 1)
+    all_meta = send(meta_r.at[others], meta_r.at[others], ms_sem.at[0], mr_sem.at[0], dp=mate_dp)
+
+    def spot(s, k, h):
+        return 2 * n - 1 + k // 2 - 1 if h else s * n + k - 1
 
     def row_copies(t, s, k, halves=(0, 1)):
-        sems = lambda h: (gs_sem.at[t, s, k, h], gr_sem.at[t, s, k, h])
+        sems = lambda h: (gs_sem.at[t, spot(s, k, h)], gr_sem.at[t, spot(s, k, h)])
         landed = rows_r.at[t, s, k]
         if s == 0:
             if k % 2 and k > 1:
@@ -119,7 +127,7 @@
         c.wait()
     pairs = [(0, k) for k in range(1, n)] + [(1, k) for k in range(n)]
     for s, k in pairs:
-        start(meta_copies(s, k))
+        meta_copy(s, k).start()
     direct = [(0, k) for k in range(2, n, 2)] + [(1, 0), (0, 1)]
     for t in range(2):
         for s, k in direct:
@@ -135,18 +143,16 @@
     padded = -(-local // 8) * 8
 
     def route(s, k):
-        if s or k:
-            landed(meta_copies(s, k))
-        iv, gv = ids_r[s, k], gates_r[s, k]
+        mv = meta_r[s * n + k]
         count, first = (part, me * local + mine) if s else (local, me * local)
         hots, values = (hot1, slot_gate1) if s else (hot, slot_gate)
         expert = lax.broadcasted_iota(jnp.int32, (padded, tokens), 0) + first
         hit = jnp.zeros((padded, tokens), F32)
         gate = jnp.zeros((padded, tokens), F32)
         for c in range(top):
-            same = iv[c : c + 1] == expert
+            same = mv[c : c + 1] == expert
             hit = hit + jnp.where(same, 1.0, 0.0)
-            gate = gate + jnp.where(same, gv[c : c + 1].astype(F32) * (1.0 / 65536.0), 0.0)
+            gate = gate + jnp.where(same, mv[top + c : top + c + 1].astype(F32) * (1.0 / 65536.0), 0.0)
         rank = dot(hit.astype(BF), before)
         rank = jnp.where(hit > 0.5, rank, -1.0)
         slot = lax.broadcasted_iota(jnp.int32, (cap, tokens), 0).astype(F32)
@@ -169,23 +175,21 @@
     def x_copy(i, a, k):
         zz = flipped(my_z, k)
         return send(
-            parts.at[other_x, i, a, zz], x_r.at[i, a, zz], xs_sem.at[i, a, k], xr_sem.at[i, a, k], dp=partner_dp
+            parts.at[other_x, i, a, zz], x_r.at[i, a, zz], xs_sem.at[0], xr_sem.at[i, a, k], dp=partner_dp
         )
 
     def z_copy(k, i, a):
         there = flipped(my_z, k)
         return send(
-            z_s.at[i, a, there], z_r.at[k, i, a], zs_sem.at[k, i, a], zr_sem.at[k, i, a],
+            z_s.at[i, a, there], z_r.at[i, a, k], zs_sem.at[0], zr_sem.at[i, a],
             dp=there * inner + my_x,
         )
 
-    def put(i, a, value):
-        for zz in range(outer):
+    def put(i, a, half, value):
+        for zz in range(outer // 2):
             for xx in range(inner):
                 at = (zz * inner + xx) * rows
-                parts[xx, i, a, zz] = value[at : at + rows].astype(BF)
-        for k in range(outer - 1, 1, -1):
-            x_copy(i, a, k).start()
+                parts[xx, i, a, half * (outer // 2) + zz] = value[at : at + rows].astype(BF)
 
     def grads(hidden_grad, p, into, e):
         pre_gate, pre_up = p[:, :ff], p[:, ff:]
@@ -219,7 +223,11 @@
         return carry
 
     def y_copy(j, k):
-        return send(rows_r.at[j, 0, k], y_r.at[j, k], ys_sem.at[j, k], yr_sem.at[j, k], expert=flipped(me, k))
+        return send(rows_r.at[j, 0, k], y_r.at[j, k], ys_sem.at[j], yr_sem.at[j], expert=flipped(me, k))
+
+    def y_all(j):
+        away = pl.ds(1, n - 1)
+        return send(y_r.at[j, away], y_r.at[j, away], ys_sem.at[j], yr_sem.at[j], dp=mate_dp)
 
     def spread(j, k):
         src = (ys, ds)[j]
@@ -233,15 +241,15 @@
             y_copy(j, k).start()
 
     def act_copy(j):
-        return pltpu.make_async_copy(act_s.at[j], act_o.at[j], out_sem.at[j])
+        return pltpu.make_async_copy(act_s.at[j], act_o.at[j], out_sem.at[0])
 
     def grad_copy(a, i):
-        return pltpu.make_async_copy(grad_s.at[a, i], grad_o.at[a, i], out_sem.at[2 + a * local + i])
+        return pltpu.make_async_copy(grad_s.at[a, i], grad_o.at[a, i], out_sem.at[1])
 
     def returned(j):
         total = spread(j, 0)
+        y_all(j).wait_recv()
         for k in range(1, n):
-            y_copy(j, k).wait_recv()
             total = total + y_r[j, k].astype(F32)
         act_s[j] = total.astype(BF)
         act_copy(j).start()
@@ -254,12 +262,12 @@
             z_copy(k, i, a).start()
 
     def finish(i, a):
+        far_z = pl.ds(1, outer - 1)
+        send(z_r.at[i, a, far_z], z_r.at[i, a, far_z], zs_sem.at[0], zr_sem.at[i, a], dp=mate_dp).wait_recv()
         for first, e in ((0, mine + i), (1, part - mine + i)):
             total = 0.0
             for k in range(first, outer, 2):
-                if k:
-                    z_copy(k, i, a).wait_recv()
-                total = total + (z_r[k, i, a] if k else z_s[i, a, my_z]).astype(F32)
+                total = total + (z_r[i, a, k] if k else z_s[i, a, my_z]).astype(F32)
             grad_s[a, e] = total * scale
             grad_copy(a, e).start()
 
@@ -297,6 +305,7 @@
     route(0, 0)
     for t in range(2):
         take(t, 0, 0)
+    all_meta.wait_recv()
     for s, k in pairs:
         route(s, k)
     for t in range(2):
@@ -315,63 +324,78 @@
     lax.fori_loop(0, part, forward_pair, 0)
     far_first(1)
     lax.fori_loop(part - mine, local - mine, backward, 0)
+    cut = d_model // 2
+    near = lax.div(my_z, outer // 2)
+
+    def columns(ref, i, half):
+        return ref[i, :, pl.ds(pl.multiple_of(half * cut, cut), cut)]
+
+    def own_down(i, half):
+        return dot(columns(gs, mine + i, half), hs[mine + i], 0, 0)
+
+    def put_down(i, half, seed):
+        put(i, 2, half, seed + dot(columns(gs1, i, half), hs1[i], 0, 0))
+
+    def put_both(i, half):
+        both = dot(columns(xs, mine + i, half), gu[mine + i], 0, 0) + dot(columns(xs1, i, half), gu1[i], 0, 0)
+        put(i, 0, half, both[:, :ff])
+        put(i, 1, half, both[:, ff:])
+
+    def x_start(i, a, ks):
+        for k in ks:
+            x_copy(i, a, k).start()
+
+    order = (2, 0, 1)
+    chunks = [(i, a) for i in range(part) for a in order]
+    far_ks = range(outer - 1, outer // 2 - 1, -1)
+    near_ks = range(outer // 2 - 1, 0, -1)
+
+    seed = own_down(0, 1 - near)
     far_last(1)
-
-    order = (2, 0, 1)
     for i in range(part):
-        e = mine + i
-        put(i, 2, dot(gs[e], hs[e], 0, 0) + dot(gs1[i], hs1[i], 0, 0))
-        grads(dot(gs1[i], wd[e]), pre[e], gu1, i)
+        put_down(i, 1 - near, seed if i == 0 else own_down(i, 1 - near))
+        x_start(i, 2, far_ks)
+        grads(dot(gs1[i], wd[mine + i]), pre[mine + i], gu1, i)
         if i == part - 1:
-            for k in range(outer - 1, 1, -1):
+            for k in far_ks:
                 x_stage(0, 2, k)
-        both = dot(xs[e], gu[e], 0, 0) + dot(xs1[i], gu1[i], 0, 0)
-        put(i, 0, both[:, :ff])
-        put(i, 1, both[:, ff:])
-
-    for k in (1, 0):
-        for i in range(part):
-            for a in order:
-                x_copy(i, a, k).start()
+        put_both(i, 1 - near)
+        x_start(i, 0, far_ks)
+        x_start(i, 1, far_ks)
+    for i in range(part):
+        put_down(i, near, own_down(i, near))
+        put_both(i, near)
+        for a in order:
+            x_start(i, a, near_ks)
+        for k in far_ks:
+            x_stage(*chunks[1 + i], k)
+    for i, a in chunks:
+        x_start(i, a, (0,))
     back_out(1)
-    for i in range(part):
-        for a in order:
-            if i or a != 2:
-                for k in range(outer - 1, 1, -1):
-                    x_stage(i, a, k)
+    for i, a in chunks[1 + part :]:
+        for k in far_ks:
+            x_stage(i, a, k)
     returned(0)
-    for i in range(part):
-        for a in order:
-            x_stage(i, a, 1)
+    for i, a in chunks:
+        for k in near_ks:
+            x_stage(i, a, k)
     returned(1)
-    for i in range(part):
-        for a in order:
-            x_stage(i, a, 0)
-            finish(i, a)
-
+    for i, a in chunks:
+        x_stage(i, a, 0)
+        finish(i, a)
+
+    all_meta.wait_send()
     for s, k in pairs:
-        left(meta_copies(s, k))
         for t in range(2):
             if s or k < 2 or k % 2 == 0:
                 left(row_copies(t, s, k, (1,)))
     for j in range(2):
-        for k in range(1, n):
-            y_copy(j, k).wait_send()
-
-    def drain(i, carry):
-        for a in range(3):
-            for k in range(outer):
-                x_copy(i, a, k).wait_send()
-                if k:
-                    z_copy(k, i, a).wait_send()
-        return carry
-
-    lax.fori_loop(0, part, drain, 0)
-    for j in range(2):
-        act_copy(j).wait()
-    for a in range(3):
-        for e in range(local):
-            grad_copy(a, e).wait()
+        y_all(j).wait_send()
+    send(parts.at[other_x], x_r, xs_sem.at[0], xr_sem.at[0, 0, 0], dp=partner_dp).wait_send()
+    sent = z_r.at[:, :, pl.ds(1, outer - 1)]
+    send(sent, sent, zs_sem.at[0], zr_sem.at[0, 0], dp=mate_dp).wait_send()
+    pltpu.make_async_copy(act_s, act_o, out_sem.at[0]).wait()
+    pltpu.make_async_copy(grad_s, grad_o, out_sem.at[1]).wait()
 
 
 def write(act, grad, out_o, din_o, gg_o, gu_o, gd_o, sem):
@@ -413,8 +437,7 @@
         pltpu.VMEM((3, local, rows, ff), F32),
         pltpu.VMEM((local, d_model, 2 * ff), BF),
         pltpu.VMEM((local, d_model, ff), BF),
-        pltpu.VMEM((2, n, top, count), jnp.int32),
-        pltpu.VMEM((2, n, top, count), jnp.int32),
+        pltpu.VMEM((2 * n, 2 * top, count), jnp.int32),
         pltpu.VMEM((2, 2, n, count, d_model), BF),
         pltpu.VMEM((n, local * cap, count), BF),
         pltpu.VMEM((n, part * cap, count), BF),
@@ -435,7 +458,7 @@
         pltpu.VMEM((inner, part, 3, outer, rows, ff), BF),
         pltpu.VMEM((part, 3, outer, rows, ff), BF),
         pltpu.VMEM((part, 3, outer, rows, ff), BF),
-        pltpu.VMEM((outer, part, 3, rows, ff), BF),
+        pltpu.VMEM((part, 3, outer, rows, ff), BF),
     ]
     args = (expert_ids.T, gate_fixed.T, tokens, cotangent, w_gate, w_up, w_down)
     act, grad = pl.pallas_call(
@@ -447,12 +470,12 @@
         in_specs=[hbm] * 7,
         out_specs=(hbm,) * 2,
         scratch_shapes=buffers + [
-            dma((3,)), dma((4,)), dma((2 + 3 * local,)),
-            dma((2, 2, n)), dma((2, 2, n)),
-            dma((2, 2, n, 2)), dma((2, 2, n, 2)),
-            dma((2, n)), dma((2, n)),
-            dma((part, 3, outer)), dma((part, 3, outer)),
-            dma((outer, part, 3)), dma((outer, part, 3)),
+            dma((3,)), dma((4,)), dma((2,)),
+            dma((1,)), dma((1,)),
+            dma((2, 2 * n - 1 + n // 2 - 1)), dma((2, 2 * n - 1 + n // 2 - 1)),
+            dma((2,)), dma((2,)),
+            dma((1,)), dma((part, 3, outer)),
+            dma((1,)), dma((part, 3)),
         ],
         compiler_params=pltpu.CompilerParams(
             collective_id=0,

time: 83.9 us -> 82.4 us (0.982)
  Pallas kernels: 83 us -> 81.4 us
    pallas_call x1, Pallas kernels: 81.5 us -> 79.9 us  [shards(): pl.pallas_call(functools.partial(kernel, n, inner, outer, top, scale), ou...]
where the time goes in v3:
time: 82.4 us; the launch traced here: 82.2 us
  Pallas kernels  81.4 us (99%)
    pallas_call x1, Pallas kernels, shards(): pl.pallas_call(functools.partial(kernel, n, inner, outer, top, scale), ou...  79.9 us

profile of v3, /device:TPU:0, one launch (start us, length us, event | category | flops | bytes accessed | tf_op | source)
XLA Modules:
  0.0 82.2 jit_solution(12409263756125046165)
XLA Ops:
  0.6 79.9 %shard_map.110 = (bf16[2,256,768]{2,1,0:T(8,128)(2,1)S(1)}, f32[3,4,96,384]{3,2,1,0:T(8,128)S(1)}) custom-call(s32[2,256]{1,0:T(2,128)} %bitcast.2, s32[2,256]{1,0:T(2,128)} %bitcast.3, bf16[256,768]{1,0:T(8,128)(2,1)} %tok_h.1, bf16[256,768]{1,0:T(8,128)(2,1)} %cot_h.1, bf16[4,768,384]{2,1,0:T(8,128)(2,1)} %wg_h.1, bf16[4,768,384]{2,1,0:T(8,128)(2,1)} %wu_h.1, ...), custom_call_target="tpu_custom_call" | custom-call | tf_op jit(solution)/shard_map/pallas_call | solution.py:464
  80.5 1.5 %shard_map.111 = (bf16[256,768]{1,0:T(8,128)(2,1)}, bf16[256,768]{1,0:T(8,128)(2,1)}, f32[4,96,384]{2,1,0:T(8,128)}, f32[4,96,384]{2,1,0:T(8,128)}, f32[4,96,384]{2,1,0:T(8,128)}) custom-call(bf16[2,256,768]{2,1,0:T(8,128)(2,1)S(1)} %get-tuple-element.7.act, f32[3,4,96,384]{3,2,1,0:T(8,128)S(1)} %get-tuple-element.8.grad), custom_call_target="tpu_custom_call" | custom-call | tf_op jit(solution)/shard_map/pallas_call | solution.py:488
